TPU v7x, 256 devices: a whole 4x4x8 slice. The times are simulated.
256 devices in a mesh: seq: 32 (over z_hi, y, core), fsdp: 8 (over z_lo, x).
Axes of the slice: x: 4, y: 4, z: 8 (z_hi: 4, z_lo: 2; z = z_hi * 2 + z_lo), core: 2. Of those that a mesh axis runs over, the one named last changes fastest.
Arguments:
- tokens: bfloat16 [32768, 1280], P('seq'), may hold values from -64 to 64
- cotangent: bfloat16 [32768, 1280], P('seq'), may hold values from -6 to 6
- raster_dest: int32 [32768], P('seq'), may hold values from 0 to 32767, as said below
- keep_mask: int32 [512, 16, 4096], P('seq', 'fsdp'), may hold values 0 or 1
- qkv_weight: bfloat16 [1280, 3840], P('seq', 'fsdp'), may hold values from -0.15625 to 0.15625
- out_weight: bfloat16 [1280, 1280], P('seq', 'fsdp'), may hold values from -0.15625 to 0.15625
Outputs:
- attended: bfloat16 [32768, 1280], P('seq', 'fsdp')
- grad_tokens: bfloat16 [32768, 1280], P('seq', 'fsdp')
- grad_qkv: float32 [1280, 3840], P('seq', 'fsdp')
- grad_out: float32 [1280, 1280], P('seq', 'fsdp')
Inputs may be any that keep to these rules, and one draw needn't show every extreme that they name: `raster_dest`: A permutation. Raster rows form bands of 2048 rows (8 patch rows of 256 patches); band b holds 32 windows of 8 by 8 patches, which go one to each block of 1024 window-order rows, in an order drawn for each band; inside its block, band b's window takes rows b * 64 to (b + 1) * 64 - 1, its patches in raster order.
All inputs are finite; a program needn't handle non-finite values. No bound on the sum of `keep_mask` on one device may be relied on, other than what follows from the above.
Results may differ from a plain program's by a relative error of at most 0.025.
The roundings to bfloat16 on the way count: a program that leaves them out, or rounds other values in their place, can miss the bound.
Values may be sent and summed in bfloat16 or wider, within the bound.
No kernel may reach another device: no remote copies, remote signals or barrier semaphores. Data moves between devices by JAX's collectives and lax.ppermute only.
A program may use at most 64 MiB of HBM per device.

v0:
```python
import jax
import jax.numpy as jnp
from jax import lax
from jax.sharding import PartitionSpec as P

HEAD_DIM = 80
WIN = 8
WIN_TOK = 64


INV_KEEP = 1.0 / 0.9


def to_half(values):
    return lax.optimization_barrier(values.astype(jnp.bfloat16))


def head_total(partial_value):
    rounded = to_half(partial_value).astype(jnp.float32)
    return lax.psum_scatter(
        rounded.astype(jnp.bfloat16), "fsdp", scatter_dimension=1, tiled=True
    ).astype(jnp.float32)


def per_device(tokens, cotangent, raster_dest, keep_mask, qkv_weight, out_weight):
    seq_count = lax.axis_size("seq")
    tok_dev = tokens.shape[0]
    score_scale = HEAD_DIM ** (-0.5)
    windows_local = tok_dev // WIN_TOK
    heads_local = keep_mask.shape[1]
    send_order = jnp.argsort(raster_dest)
    back_order = jnp.argsort(send_order)
    slot_index = jnp.arange(tok_dev, dtype=jnp.int32)
    band_index = slot_index // WIN_TOK
    patch_row = slot_index % WIN_TOK // WIN
    source = (band_index * WIN_TOK * seq_count + patch_row * WIN * seq_count) // tok_dev
    recv_slot = jnp.argsort(source * tok_dev + slot_index)
    slot_recv = jnp.argsort(recv_slot)

    def restore(window_rows):
        outgoing = window_rows[recv_slot]
        returned = lax.all_to_all(outgoing, "seq", split_axis=0, concat_axis=0, tiled=True)
        return returned[back_order]

    qkv_full, out_full = (
        lax.all_gather(qkv_weight, "seq", axis=0, tiled=True),
        lax.all_gather(out_weight, "seq", axis=0, tiled=True),
    )
    windowed = lax.all_to_all(tokens[send_order], "seq", split_axis=0, concat_axis=0, tiled=True)[
        slot_recv
    ]
    cot_window = lax.all_to_all(
        cotangent[send_order], "seq", split_axis=0, concat_axis=0, tiled=True
    )[slot_recv]
    projected = jnp.dot(windowed, qkv_full, preferred_element_type=jnp.float32).astype(jnp.bfloat16)
    unpacked = projected.reshape(windows_local, WIN_TOK, heads_local, 3, HEAD_DIM)
    queries = unpacked[:, :, :, 0].transpose(0, 2, 1, 3)
    key_rows = unpacked[:, :, :, 1].transpose(0, 2, 1, 3)
    value_rows = unpacked[:, :, :, 2].transpose(0, 2, 1, 3)
    keep_scale = (
        keep_mask.reshape(windows_local, heads_local, WIN_TOK, WIN_TOK).astype(jnp.float32)
        * INV_KEEP
    )
    scores = (
        jnp.einsum("whqe,whke->whqk", queries, key_rows, preferred_element_type=jnp.float32)
        * score_scale
    )
    attn_probs = jax.nn.softmax(scores, axis=-1)
    dropped = (attn_probs * keep_scale).astype(jnp.bfloat16)
    mixed = jnp.einsum(
        "whqk,whke->whqe", dropped, value_rows, preferred_element_type=jnp.float32
    ).astype(jnp.bfloat16)
    mixed_heads = mixed.transpose(0, 2, 1, 3).reshape(tok_dev, heads_local * HEAD_DIM)
    contract = (((1,), (1,)), ((), ()))
    out_partial = lax.dot_general(
        mixed_heads, out_full, contract, preferred_element_type=jnp.float32
    )
    attended = restore(head_total(out_partial).astype(jnp.bfloat16))
    grad_heads = jnp.dot(cot_window, out_full, preferred_element_type=jnp.float32).astype(
        jnp.bfloat16
    )
    grad_rows = grad_heads.reshape(windows_local, WIN_TOK, heads_local, HEAD_DIM).transpose(
        0, 2, 1, 3
    )
    grad_probs = (
        jnp.einsum("whqe,whke->whqk", grad_rows, value_rows, preferred_element_type=jnp.float32)
        * keep_scale
    )
    inner = jnp.sum(grad_probs * attn_probs, axis=-1, keepdims=True)
    grad_scores = (score_scale * attn_probs * (grad_probs - inner)).astype(jnp.bfloat16)
    grad_query = jnp.einsum(
        "whqk,whke->whqe", grad_scores, key_rows, preferred_element_type=jnp.float32
    )
    grad_key = jnp.einsum(
        "whqk,whqe->whke", grad_scores, queries, preferred_element_type=jnp.float32
    )
    grad_value = jnp.einsum(
        "whqk,whqe->whke", dropped, grad_rows, preferred_element_type=jnp.float32
    )
    stacked = jnp.stack([grad_query, grad_key, grad_value], axis=3)
    grad_projected = (
        stacked.transpose(0, 2, 1, 3, 4)
        .reshape(tok_dev, 3 * heads_local * HEAD_DIM)
        .astype(jnp.bfloat16)
    )
    back_partial = lax.dot_general(
        grad_projected, qkv_full, contract, preferred_element_type=jnp.float32
    )
    grad_tokens = restore(head_total(back_partial).astype(jnp.bfloat16))
    over_rows = (((0,), (0,)), ((), ()))
    grad_qkv_local = lax.dot_general(
        windowed, grad_projected, over_rows, preferred_element_type=jnp.float32
    )
    grad_out_local = lax.dot_general(
        cot_window, mixed_heads, over_rows, preferred_element_type=jnp.float32
    )
    grad_qkv, grad_out = (
        lax.psum_scatter(grad_qkv_local, "seq", scatter_dimension=0, tiled=True),
        lax.psum_scatter(grad_out_local, "seq", scatter_dimension=0, tiled=True),
    )
    grad_scale = (tok_dev * seq_count) ** (-0.5)
    return (attended, grad_tokens, grad_qkv * grad_scale, grad_out * grad_scale)


def solution(mesh):
    return jax.shard_map(
        per_device,
        mesh=mesh,
        in_specs=(
            P("seq", None),
            P("seq", None),
            P("seq"),
            P("seq", "fsdp", None),
            P("seq", "fsdp"),
            P("seq", "fsdp"),
        ),
        out_specs=(P("seq", "fsdp"), P("seq", "fsdp"), P("seq", "fsdp"), P("seq", "fsdp")),
        check_vma=False,
    )
```

profile of v0, /device:TPU:1, one launch (start us, length us, event | category | flops | bytes accessed | tf_op | source)
XLA Modules:
  0.0 582.6 jit_solution(13186685068350491355)
XLA Ops:
  7.2 5.2 sort.59
  12.4 5.5 gather_fusion.4
  17.9 12.8 %all-to-all-start.2 = ((bf16[32,32,1280]{2,1,0:T(8,128)(2,1)}), bf16[32,32,1280]{2,1,0:T(8,128)(2,1)}, u32[]{:S(2)}, u32[]{:S(2)}) async-start(bf16[32,32,1280]{2,1,0:T(8,128)(2,1)} %bitcast.90), calls=%async_computation.2 | async-start | bytes 5242880 | tf_op jit(solution)/shard_map/all_to_all | solution.py:52
  30.7 8.7 %gather_fusion = bf16[1024,1280]{1,0:T(8,128)(2,1)} fusion(bf16[1024,1280]{1,0:T(8,128)(2,1)} %param.6, s32[1024]{0:T(1024)S(1)} %fusion.29), kind=kCustom, calls=%fused_computation | custom fusion | bytes 5246976 | tf_op jit(solution)/shard_map/gather | solution.py:49
  39.4 52.9 %all-to-all-done.2 = bf16[32,32,1280]{2,1,0:T(8,128)(2,1)} async-done(((bf16[32,32,1280]{2,1,0:T(8,128)(2,1)}), bf16[32,32,1280]{2,1,0:T(8,128)(2,1)}, u32[]{:S(2)}, u32[]{:S(2)}) %all-to-all-start.2) | async-done | bytes 2621472 | tf_op jit(solution)/shard_map/all_to_all | solution.py:52
  92.3 5.8 all-to-all-start
  98.2 0.7 all-gather.2.cloned.1.call-update
  98.9 1.3 convert_multiply_fusion
  100.3 1.6 reshape.113
  101.9 2.6 copy.35
  104.5 4.4 sort.60
  108.8 4.4 sort.61
  113.2 88.0 %all_gather.7 = bf16[1280,160]{1,0:T(8,128)(2,1)S(1)} all-gather(bf16[40,160]{1,0:T(8,128)(2,1)S(1)} %copy-done.8), channel_id=1, replica_groups=mesh['seq'=32,'fsdp'=8] {'seq'}, dimensions={0}, use_global_device_ids=true | all-gather | bytes 422400 | tf_op jit(solution)/shard_map/all_gather | solution.py:47
  201.2 8.8 %gather_fusion.5 = bf16[1024,1280]{1,0:T(8,128)(2,1)} fusion(bf16[1024,1280]{1,0:T(8,128)(2,1)} %bitcast.12, s32[1024]{0:T(1024)S(1)} %fusion.30), kind=kCustom, calls=%fused_computation.5 | custom fusion | bytes 5246976 | tf_op jit(solution)/shard_map/gather | solution.py:52
  210.0 3.5 convolution_convert_fusion.7
  213.5 2.3 reshape.36
  215.8 2.4 copy.39
  218.3 8.7 %gather_fusion.1 = bf16[1024,1280]{1,0:T(8,128)(2,1)} fusion(bf16[1024,1280]{1,0:T(8,128)(2,1)} %bitcast.1, s32[1024]{0:T(1024)S(1)} %fusion.30), kind=kCustom, calls=%fused_computation.1 | custom fusion | bytes 5246976 | tf_op jit(solution)/shard_map/gather | solution.py:49
  226.9 4.5 convolution_convert_fusion.2
  231.5 3.8 reshape.34
  235.3 2.9 fusion.45
  238.2 2.4 copy.56
  240.6 2.4 copy.55
  243.1 2.4 copy.54
  245.5 2.7 fusion.46
  248.2 2.4 multiply_reduce_fusion
  250.6 0.4 multiply_convert_fusion
  251.1 0.6 copy-done.5
  251.7 0.3 fusion.5
  252.0 0.3 fusion.4
  252.3 0.1 copy-done.3
  252.4 0.3 fusion.6
  252.7 1.6 maximum_bitcast_fusion
  254.3 4.2 copy.43
  258.5 3.9 convert_element_type.53
  262.4 4.8 convolution_convert_fusion
  267.2 4.5 copy.50
  271.7 0.0 reduce-scatter.13.cloned.1.call-start
  271.8 2.3 fusion.3
  274.1 2.4 copy.38
  276.5 2.3 reshape.35
  278.8 3.4 convolution_convert_fusion.1
  282.2 4.5 copy.48
  286.7 0.0 reduce-scatter.11.cloned.1.call-start
  286.8 0.9 copy-done.6
  287.7 3.7 fusion.52
  291.5 5.1 fusion.51
  296.6 16.5 %reduce-scatter.15.cloned.1.call-done = bf16[160,1024]{1,0:T(8,128)(2,1)} async-done(((bf16[1280,1024]{1,0:T(8,128)(2,1)}), bf16[160,1024]{1,0:T(8,128)(2,1)}) %reduce-scatter.15.cloned.1.call-update) | async-done | bytes 327696
  313.2 1.2 copy.51
  314.3 4.9 gather_fusion.6
  319.3 13.8 %all-to-all-start.3 = ((bf16[32,32,160]{2,1,0:T(8,128)(2,1)}), bf16[32,32,160]{2,1,0:T(8,128)(2,1)S(1)}, u32[]{:S(2)}, u32[]{:S(2)}) async-start(bf16[32,32,160]{2,1,0:T(8,128)(2,1)} %bitcast.95), calls=%async_computation.3 | async-start | bytes 1048576 | tf_op jit(solution)/shard_map/all_to_all | solution.py:42
  333.1 4.4 sort.62
  337.5 34.0 %reduce-scatter.13.cloned.1.call-done = bf16[160,1024]{1,0:T(8,128)(2,1)} async-done(((bf16[1280,1024]{1,0:T(8,128)(2,1)}), bf16[160,1024]{1,0:T(8,128)(2,1)}) %reduce-scatter.13.cloned.1.call-update) | async-done | bytes 327696
  371.5 2.0 copy.49
  373.5 5.7 gather_fusion.2
  379.2 13.0 %all-to-all-start.1 = ((bf16[32,32,160]{2,1,0:T(8,128)(2,1)}), bf16[32,32,160]{2,1,0:T(8,128)(2,1)}, u32[]{:S(2)}, u32[]{:S(2)}) async-start(bf16[32,32,160]{2,1,0:T(8,128)(2,1)} %bitcast.94), calls=%async_computation.1 | async-start | bytes 1048576 | tf_op jit(solution)/shard_map/all_to_all | solution.py:42
  392.3 74.3 %reduce-scatter.11.cloned.1.call-done = f32[40,160]{1,0:T(8,128)} async-done(((f32[1280,160]{1,0:T(8,128)}), f32[40,160]{1,0:T(8,128)}) %reduce-scatter.11.cloned.1.call-update) | async-done | bytes 25616 | tf_op jit(solution)/shard_map/reduce_scatter | solution.py:119
  466.6 1.4 broadcast_multiply_fusion.1
  468.0 94.2 %reduce-scatter.9.cloned.1.call-done = f32[40,480]{1,0:T(8,128)} async-done(((f32[1280,480]{1,0:T(8,128)}), f32[40,480]{1,0:T(8,128)}) %reduce-scatter.9.cloned.1.call-update) | async-done | bytes 76816 | tf_op jit(solution)/shard_map/reduce_scatter | solution.py:118
  562.2 1.5 broadcast_multiply_fusion
  563.7 4.9 gather_fusion.7
  568.6 1.9 copy.45
  570.6 4.6 gather_fusion.3
  575.2 0.9 copy.44
  (35 shorter events, 0.3 us)
Async XLA Ops:
  7.2 5.2 copy-start
  17.9 74.4 %all-to-all-start.2 = ((bf16[32,32,1280]{2,1,0:T(8,128)(2,1)}), bf16[32,32,1280]{2,1,0:T(8,128)(2,1)}, u32[]{:S(2)}, u32[]{:S(2)}) async-start(bf16[32,32,1280]{2,1,0:T(8,128)(2,1)} %bitcast.90), calls=%async_computation.2 | async-start | bytes 5242880 | tf_op jit(solution)/shard_map/all_to_all | solution.py:52
  92.3 126.0 %all-to-all-start = ((bf16[32,32,1280]{2,1,0:T(8,128)(2,1)}), bf16[32,32,1280]{2,1,0:T(8,128)(2,1)}, u32[]{:S(2)}, u32[]{:S(2)}) async-start(bf16[32,32,1280]{2,1,0:T(8,128)(2,1)} %bitcast.89), calls=%async_computation | async-start | bytes 5242880 | tf_op jit(solution)/shard_map/all_to_all | solution.py:49
  98.1 15.1 %copy-start.8 = (bf16[40,160]{1,0:T(8,128)(2,1)S(1)}, bf16[40,160]{1,0:T(8,128)(2,1)}, u32[]{:S(2)}) copy-start(bf16[40,160]{1,0:T(8,128)(2,1)} %param.11) | copy-start | bytes 38404
  98.1 128.8 %all-gather.2.cloned.1.call-start = ((), (), s32[]{:S(2)}) async-start(), calls=%async_computation.8 | async-start | bytes 1351680 | tf_op jit(solution)/shard_map/all_gather | solution.py:46
  98.9 214.3 %reduce-scatter.15.cloned.1.call-start = ((), (), s32[]{:S(2)}) async-start(), calls=%async_computation.12 | async-start | bytes 2949120
  248.2 2.5 copy-start.2
  248.2 2.5 copy-start.7
  250.6 1.1 copy-start.5
  250.6 1.3 copy-start.4
  251.1 1.2 copy-start.1
  251.1 1.3 copy-start.3
  271.7 99.8 %reduce-scatter.13.cloned.1.call-start = ((), (), s32[]{:S(2)}) async-start(), calls=%async_computation.11 | async-start | bytes 2949120
  286.7 1.0 copy-start.6
  286.7 179.9 %reduce-scatter.11.cloned.1.call-start = ((), (), s32[]{:S(2)}) async-start(), calls=%async_computation.10 | async-start | bytes 1351680 | tf_op jit(solution)/shard_map/reduce_scatter | solution.py:119
  291.4 270.7 %reduce-scatter.9.cloned.1.call-start = ((), (), s32[]{:S(2)}) async-start(), calls=%async_computation.9 | async-start | bytes 2703360 | tf_op jit(solution)/shard_map/reduce_scatter | solution.py:118
  319.3 59.9 %all-to-all-start.3 = ((bf16[32,32,160]{2,1,0:T(8,128)(2,1)}), bf16[32,32,160]{2,1,0:T(8,128)(2,1)S(1)}, u32[]{:S(2)}, u32[]{:S(2)}) async-start(bf16[32,32,160]{2,1,0:T(8,128)(2,1)} %bitcast.95), calls=%async_computation.3 | async-start | bytes 1048576 | tf_op jit(solution)/shard_map/all_to_all | solution.py:42
  379.2 191.4 %all-to-all-start.1 = ((bf16[32,32,160]{2,1,0:T(8,128)(2,1)}), bf16[32,32,160]{2,1,0:T(8,128)(2,1)}, u32[]{:S(2)}, u32[]{:S(2)}) async-start(bf16[32,32,160]{2,1,0:T(8,128)(2,1)} %bitcast.94), calls=%async_computation.1 | async-start | bytes 1048576 | tf_op jit(solution)/shard_map/all_to_all | solution.py:42
Sparse Core Ops, SparseCore 0:
  101.5 68.5 all-gather.1
  271.9 41.2 reduce-scatter.14
  315.7 55.7 reduce-scatter.12
  375.2 91.3 reduce-scatter.10
  470.8 91.3 reduce-scatter.8
where the time goes:
time: 585 us; the launch traced here: 583 us
  waiting for transfers between devices  273 us (47%)
  local copies, waits for them, and re-layouts  104 us (18%)
  blocking collectives  88 us (15%)
  starting transfers between devices  45.7 us (8%)
  matrix products  33.5 us (6%)
  other arithmetic  24.6 us (4%)
  between operations  14 us (2%)
    reduce_scatter x1, waiting for transfers between devices, per_device(): lax.psum_scatter(grad_qkv_local, 'seq', scatter_dimension=0, tiled=True)  94.2 us
    all_gather x1, blocking collectives, per_device(): lax.all_gather(out_weight, 'seq', axis=0, tiled=True)  88 us
    reduce_scatter x1, waiting for transfers between devices, per_device(): lax.psum_scatter(grad_out_local, 'seq', scatter_dimension=0, tiled=True)  74.3 us
    all_to_all x1, waiting for transfers between devices, per_device(): lax.all_to_all(cotangent[send_order], 'seq', split_axis=0, concat_axis=0,...  52.9 us
    unnamed x7, waiting for transfers between devices  51.3 us
    all_to_all x2, starting transfers between devices, restore(): lax.all_to_all(outgoing, 'seq', split_axis=0, concat_axis=0, tiled=True)  26.9 us
    unnamed x27, local copies, waits for them, and re-layouts  23.8 us
    all_to_all x1, starting transfers between devices, per_device(): lax.all_to_all(cotangent[send_order], 'seq', split_axis=0, concat_axis=0,...  12.8 us
  transfers between devices with their start and end apart: 9, of which 5 were waited for; matrix products, arithmetic and copies ran while one was open for 17% of the time, Pallas kernels for 0%

commit v1 on v0

v1 whole, which is shorter than its diff:
```python
import functools

import jax
import jax.numpy as jnp
from jax import lax
from jax.experimental import pallas as pl
from jax.experimental.pallas import tpu as pltpu
from jax.sharding import Mesh
from jax.sharding import PartitionSpec as P

D = 1280
HEAD_DIM = 80
WIN_TOK = 64
TOK_DEV = 1024
PAIR = 128
INV_KEEP = 1.0 / 0.9
SCORE_SCALE = HEAD_DIM**-0.5
BF = jnp.bfloat16
F32 = jnp.float32
NT = (((1,), (1,)), ((), ()))
TN = (((0,), (0,)), ((), ()))
ANY = pl.BlockSpec(memory_space=pl.ANY)
VMEM = pl.BlockSpec(memory_space=pltpu.VMEM)
SMEM = pl.BlockSpec(memory_space=pltpu.SMEM)


def params(mib):
    return pltpu.CompilerParams(vmem_limit_bytes=mib << 20)


def cost(flops, moved):
    return pl.CostEstimate(flops=flops, bytes_accessed=moved, transcendentals=0)


def dot(a, b, dims=None):
    if dims is None:
        dims = (((1,), (0,)), ((), ()))
    return lax.dot_general(a, b, dims, preferred_element_type=F32)


def pick_kernel(idx_ref, tok_ref, cot_ref, out_ref, sems):
    row = idx_ref[16]
    copies = []
    for k in range(16):
        window = idx_ref[k]
        for a, src in enumerate((tok_ref, cot_ref)):
            copies.append(
                pltpu.make_async_copy(
                    src.at[row, window], out_ref.at[k, a], sems.at[2 * k + a]
                )
            )
    for copy in copies:
        copy.start()
    for copy in copies:
        copy.wait()


def pick(idx, tokens, cotangent):
    view = (4, 32, 8, D)
    return pl.pallas_call(
        pick_kernel,
        out_shape=jax.ShapeDtypeStruct((16, 2, 8, D), BF),
        in_specs=[SMEM, ANY, ANY],
        out_specs=ANY,
        scratch_shapes=[pltpu.SemaphoreType.DMA((32,))],
        cost_estimate=cost(0, 1 << 21),
        name="pick_rows",
    )(idx, tokens.reshape(view), cotangent.reshape(view))


def weights_kernel(idx_ref, w0, w1, w2, w3, wp_ref, op_ref, a_ref, b_ref, full, sems):
    z, y = idx_ref[0], idx_ref[1]
    copies = []
    for k, src in enumerate((w0, w1, w2, w3)):
        y_from = lax.rem(y - k + 4, 4)
        for m in range(8):
            z_from = lax.rem(z - m + 8, 8)
            slot = (z_from // 2) * 8 + y_from * 2 + lax.rem(z_from, 2)
            copies.append(
                pltpu.make_async_copy(src.at[m], full.at[slot], sems.at[8 * k + m])
            )
    for copy in copies:
        copy.start()
    for copy in copies:
        copy.wait()
    i = lax.broadcasted_iota(jnp.int32, (640, 768), 0)
    j = lax.broadcasted_iota(jnp.int32, (640, 768), 1)
    spread = jnp.where((j % 128 < HEAD_DIM) & (i == j // 128 * HEAD_DIM + j % 128), 1.0, 0.0)
    spread = spread.astype(BF)
    i = lax.broadcasted_iota(jnp.int32, (640, 256), 0)
    j = lax.broadcasted_iota(jnp.int32, (640, 256), 1)
    spread_out = jnp.where(
        (j % 128 < HEAD_DIM) & (i == 480 + j // 128 * HEAD_DIM + j % 128), 1.0, 0.0
    ).astype(BF)
    for r in range(4):
        rows = full[8 * r : 8 * r + 8].reshape(320, 640)
        wp_ref[pl.ds(320 * r, 320), :] = dot(rows, spread).astype(BF)
        op_ref[pl.ds(320 * r, 320), :] = dot(rows, spread_out).astype(BF)
    for g in range(4):
        lo, hi = g * 160, (4 + g) * 160
        a_ref[g, 0:160, :] = op_ref[lo : lo + 160, :]
        a_ref[g, 160:256, :] = jnp.zeros((96, 256), BF)
        a_ref[g, 256:416, :] = op_ref[hi : hi + 160, :]
        a_ref[g, 416:512, :] = jnp.zeros((96, 256), BF)
        b_ref[g, 0:32, :] = jnp.zeros((32, 768), BF)
        b_ref[g, 32:192, :] = wp_ref[lo : lo + 160, :]
        b_ref[g, 192:256, :] = wp_ref[hi + 96 : hi + 160, :]
        b_ref[g, 256:288, :] = jnp.zeros((32, 768), BF)
        b_ref[g, 288:384, :] = wp_ref[hi : hi + 96, :]


def arrange_weights(idx, pieces):
    shape = jax.ShapeDtypeStruct
    return pl.pallas_call(
        weights_kernel,
        out_shape=(
            shape((D, 768), BF),
            shape((D, 256), BF),
            shape((4, 512, 256), BF),
            shape((4, 384, 768), BF),
        ),
        in_specs=[SMEM] + [ANY] * 4,
        out_specs=(VMEM,) * 4,
        scratch_shapes=[pltpu.VMEM((32, 40, 640), BF), pltpu.SemaphoreType.DMA((32,))],
        compiler_params=params(40),
        cost_estimate=cost(2 * D * 640 * 1024, 8 << 20),
        name="arrange_weights",
    )(idx, *pieces)


def layer_kernel(
    idx_ref, *refs
):
    pieces = refs[:8]
    wp_ref, op_ref, a_ref, b_ref, keep_ref = refs[8:13]
    mine = refs[13:17]
    other = refs[17:21]
    grads = refs[21:25]
    x_ref, c_ref, gp_ref, mix_ref, z_ref, g_ref, g1_ref, m1_ref, in_sems, out_sems = refs[25:]
    core, x_pos, y_pos = idx_ref[0], idx_ref[1], idx_ref[2]
    copies = []
    for half in range(2):
        for k in range(4):
            src = pieces[4 * half + k]
            which = core if half == 0 else 1 - core
            row = pl.multiple_of((4 * which + lax.rem(x_pos - k + 4, 4)) * 8, 8)
            for a, dst in enumerate((x_ref, c_ref)):
                copies.append(
                    pltpu.make_async_copy(
                        src.at[:, a], dst.at[:, pl.ds(row, 8), :], in_sems.at[2 * (4 * half + k) + a]
                    )
                )
    for copy in copies:
        copy.start()
    for copy in copies:
        copy.wait()

    row_half = lax.broadcasted_iota(jnp.int32, (PAIR, PAIR), 0) // WIN_TOK
    col_half = lax.broadcasted_iota(jnp.int32, (PAIR, PAIR), 1) // WIN_TOK
    same = row_half == col_half

    def block(i, carry):
        rows = pl.ds(pl.multiple_of(i * 256, 256), 256)
        xs = x_ref[pl.ds(4 * i, 4)].reshape(256, D)
        cs = c_ref[pl.ds(4 * i, 4)].reshape(256, D)
        projected = dot(xs, wp_ref[...]).astype(BF)
        grad_heads = dot(cs, op_ref[...]).astype(BF)
        for pair in range(2):
            lo = pair * PAIR
            for h in range(2):
                q = projected[lo : lo + PAIR, h * 384 : h * 384 + 128]
                k = projected[lo : lo + PAIR, h * 384 + 128 : h * 384 + 256]
                v = projected[lo : lo + PAIR, h * 384 + 256 : h * 384 + 384]
                g = grad_heads[lo : lo + PAIR, h * 128 : h * 128 + 128]
                scores = jnp.where(same, dot(q, k, NT) * SCORE_SCALE, -1e30)
                top = jnp.max(scores, axis=-1, keepdims=True)
                e = jnp.exp(scores - top)
                probs = e / jnp.sum(e, axis=-1, keepdims=True)
                keep = keep_ref[2 * i + pair, h].astype(F32) * INV_KEEP
                dropped = (probs * keep).astype(BF)
                mixed = dot(dropped, v).astype(BF)
                gprobs = dot(g, v, NT) * keep
                inner = jnp.sum(gprobs * probs, axis=-1, keepdims=True)
                ds = (SCORE_SCALE * probs * (gprobs - inner)).astype(BF)
                at = pl.ds(pl.multiple_of(i * 256 + lo, PAIR), PAIR)
                mix_ref[at, h * 128 : h * 128 + 128] = mixed
                gp_ref[at, h * 384 : h * 384 + 128] = dot(ds, k).astype(BF)
                gp_ref[at, h * 384 + 128 : h * 384 + 256] = dot(ds, q, TN).astype(BF)
                gp_ref[at, h * 384 + 256 : h * 384 + 384] = dot(dropped, g, TN).astype(BF)
        mixed = mix_ref[rows, :]
        grad_projected = gp_ref[rows, :]
        for k in range(4):
            group = lax.rem(x_pos + k, 4)
            out = dot(mixed, a_ref[group], NT)
            back = dot(grad_projected, b_ref[group], NT)
            at = pl.ds(4 * i, 4)
            z_ref[k, at, :, 0:128] = out[:, 0:128].astype(BF).reshape(4, 64, 128)
            z_ref[k, at, :, 128:256] = (out[:, 128:256] + back[:, 0:128]).astype(BF).reshape(4, 64, 128)
            z_ref[k, at, :, 256:384] = back[:, 128:256].astype(BF).reshape(4, 64, 128)
            z_ref[k, at, :, 384:512] = out[:, 256:384].astype(BF).reshape(4, 64, 128)
            z_ref[k, at, :, 512:640] = (out[:, 384:512] + back[:, 256:384]).astype(BF).reshape(4, 64, 128)
        return carry

    lax.fori_loop(0, 4, block, 0)

    sends = []
    for k in range(4):
        own = pl.ds(pl.multiple_of(32 * core, 32), 32)
        rest = pl.ds(pl.multiple_of(32 * (1 - core), 32), 32)
        sends.append(pltpu.make_async_copy(z_ref.at[k, :, rest, :], other[k], out_sems.at[2 * k]))
        sends.append(pltpu.make_async_copy(z_ref.at[k, :, own, :], mine[k], out_sems.at[2 * k + 1]))
    for copy in sends:
        copy.start()

    i = lax.broadcasted_iota(jnp.int32, (768, 512), 0)
    j = lax.broadcasted_iota(jnp.int32, (768, 512), 1)
    tight = jnp.where((i % 128 < HEAD_DIM) & (j == i // 128 * HEAD_DIM + i % 128), 1.0, 0.0)
    tight = tight.astype(BF)
    i = lax.broadcasted_iota(jnp.int32, (256, 256), 0)
    j = lax.broadcasted_iota(jnp.int32, (256, 256), 1)
    tight_out = jnp.where(
        (i % 128 < HEAD_DIM) & (j == 96 + i // 128 * HEAD_DIM + i % 128), 1.0, 0.0
    ).astype(BF)
    g1_ref[...] = dot(gp_ref[...], tight).astype(BF)
    m1_ref[...] = dot(mix_ref[...], tight_out).astype(BF)

    for d in range(5):
        cols = slice(256 * d, 256 * d + 256)
        ga = dot(x_ref[:, :, cols].reshape(TOK_DEV, 256), g1_ref[...], TN)
        gb = dot(c_ref[:, :, cols].reshape(TOK_DEV, 256), m1_ref[...], TN)
        g_ref[cols, 0:384] = ga[:, 0:384].astype(BF)
        g_ref[cols, 384:512] = (ga[:, 384:512] + gb[:, 0:128]).astype(BF)
        g_ref[cols, 512:640] = gb[:, 128:256].astype(BF)
    for k in range(4):
        for zh in range(4):
            start = pl.multiple_of(320 * zh + 80 * lax.rem(y_pos + k, 4), 16)
            sends.append(
                pltpu.make_async_copy(
                    g_ref.at[pl.ds(start, 80), :], grads[k].at[zh], out_sems.at[8 + 4 * k + zh]
                )
            )
            sends[-1].start()
    for copy in sends:
        copy.wait()


def layer(idx, pieces, weights, keep):
    half = jax.ShapeDtypeStruct((16, 32, 640), BF)
    quarter = jax.ShapeDtypeStruct((4, 80, 640), BF)
    outs = pl.pallas_call(
        layer_kernel,
        out_shape=(half,) * 8 + (quarter,) * 4,
        in_specs=[SMEM] + [ANY] * 8 + [VMEM] * 5,
        out_specs=(ANY,) * 12,
        scratch_shapes=[
            pltpu.VMEM((16, WIN_TOK, D), BF),
            pltpu.VMEM((16, WIN_TOK, D), BF),
            pltpu.VMEM((TOK_DEV, 768), BF),
            pltpu.VMEM((TOK_DEV, 256), BF),
            pltpu.VMEM((4, 16, WIN_TOK, 640), BF),
            pltpu.VMEM((D, 640), BF),
            pltpu.VMEM((TOK_DEV, 512), BF),
            pltpu.VMEM((TOK_DEV, 256), BF),
            pltpu.SemaphoreType.DMA((16,)),
            pltpu.SemaphoreType.DMA((24,)),
        ],
        compiler_params=params(56),
        cost_estimate=cost(12 << 30, 24 << 20),
        name="layer",
    )(idx, *pieces, *weights, keep)
    return outs[0:4], outs[4:8], outs[8:12]


def total_kernel(p0, p1, p2, p3, p4, out_ref):
    def step(w, carry):
        total = p0[w].astype(F32) + p1[w].astype(F32)
        for p in (p2, p3, p4):
            total = total + p[w].astype(F32)
        total = total.astype(BF)
        out_ref[w, 0] = total[:, 0:384]
        out_ref[w, 1, :, 0:256] = total[:, 384:640]
        out_ref[w, 1, :, 256:384] = total[:, 256:384]
        return carry

    lax.fori_loop(0, 16, step, 0)


def total(parts):
    return pl.pallas_call(
        total_kernel,
        out_shape=jax.ShapeDtypeStruct((16, 2, 32, 384), BF),
        in_specs=[VMEM] * 5,
        out_specs=VMEM,
        compiler_params=params(16),
        cost_estimate=cost(1 << 21, 4 << 20),
        name="total",
    )(*parts)


def restore_kernel(idx_ref, got_ref, att_ref, back_ref):
    z_lo = idx_ref[32]

    def step(j, carry):
        rows = got_ref[idx_ref[j]]
        last = rows[:, 256:384].astype(F32)
        last = jnp.where(z_lo == 0, last, pltpu.roll(last, 64, 1)).astype(BF)
        att = rows[:, 0:160]
        back = jnp.concatenate([rows[:, 160:256], last[:, 0:64]], axis=1)
        for r in range(4):
            at = pl.ds(pl.multiple_of(j * 8, 8), 8)
            att_ref[r, at, :] = att[8 * r : 8 * r + 8]
            back_ref[r, at, :] = back[8 * r : 8 * r + 8]
        return carry

    lax.fori_loop(0, 32, step, 0)


def restore(idx, got):
    shape = jax.ShapeDtypeStruct((4, 256, 160), BF)
    att, back = pl.pallas_call(
        restore_kernel,
        out_shape=(shape, shape),
        in_specs=[SMEM, VMEM],
        out_specs=(VMEM, VMEM),
        compiler_params=params(16),
        cost_estimate=cost(0, 2 << 20),
        name="restore",
    )(idx, got)
    return att.reshape(TOK_DEV, 160), back.reshape(TOK_DEV, 160)


def shift(value, axis, size, k):
    return lax.ppermute(value, axis, [(i, (i + k) % size) for i in range(size)])


def swap(value):
    return lax.ppermute(value, ("c", "zl"), [(0, 0), (1, 2), (2, 1), (3, 3)])


def per_device(tokens, cotangent, raster_dest, keep_mask, qkv_weight, out_weight):
    core, x_pos, y_pos = lax.axis_index("c"), lax.axis_index("x"), lax.axis_index("y")
    z_hi, z_lo = lax.axis_index("zh"), lax.axis_index("zl")
    owner = raster_dest[:256].reshape(32, 8)[:, 0] // TOK_DEV
    window = jnp.arange(32, dtype=jnp.int32)
    wanted = 2 * jnp.arange(16, dtype=jnp.int32) + z_lo
    chosen = jnp.max(jnp.where(owner[None, :] == wanted[:, None], window[None, :], 0), axis=1)
    sent = pick(jnp.concatenate([chosen, x_pos[None]]), tokens, cotangent)
    got = lax.all_to_all(sent, ("zh", "y"), split_axis=0, concat_axis=0, tiled=True)

    shard = swap(jnp.concatenate([qkv_weight, out_weight], axis=1))
    column = [shard] + [shift(shard, ("zh", "zl"), 8, k) for k in range(1, 8)]
    column = jnp.stack(column)
    quarters = [column] + [shift(column, "y", 4, k) for k in range(1, 4)]
    weights = arrange_weights(jnp.stack([2 * z_hi + z_lo, y_pos]), quarters)

    keep = swap(keep_mask.astype(BF)).reshape(8, 2, 2, WIN_TOK, WIN_TOK).transpose(0, 2, 1, 3, 4)
    zeros = jnp.zeros((8, 2, WIN_TOK, WIN_TOK), BF)
    keep = jnp.concatenate(
        [
            jnp.concatenate([keep[:, :, 0], zeros], axis=-1),
            jnp.concatenate([zeros, keep[:, :, 1]], axis=-1),
        ],
        axis=-2,
    )

    row = [got] + [shift(got, "x", 4, k) for k in range(1, 4)]
    pieces = row + [shift(piece, "c", 2, 1) for piece in row]
    mine, other, grads = layer(jnp.stack([core, x_pos, y_pos]), pieces, weights, keep)

    parts = [mine[0], shift(other[0], "c", 2, 1)]
    for k in (2, 1, 3):
        both = mine[k].astype(F32) + shift(other[k], "c", 2, 1).astype(F32)
        parts.append(shift(both.astype(BF), "x", 4, k))
    message = total(parts).reshape(32, 32, 384)
    back = lax.all_to_all(message, ("zh", "y", "zl"), split_axis=0, concat_axis=0, tiled=True)
    attended, grad_tokens = restore(jnp.concatenate([owner, z_lo[None]]), back)

    summed = grads[0].astype(F32)
    for k in range(1, 4):
        summed = summed + shift(grads[k], "y", 4, k).astype(F32)
    spread = lax.all_to_all(
        summed.astype(BF).reshape(8, 40, 640), ("zh", "zl"), split_axis=0, concat_axis=0, tiled=True
    )
    grad = swap(jnp.sum(spread.astype(F32), axis=0) * (TOK_DEV * 32) ** -0.5)
    return attended, grad_tokens, grad[:, :480], grad[:, 480:]


def solution(mesh):
    fine = Mesh(mesh.devices.reshape(4, 4, 2, 2, 4), ("zh", "y", "c", "zl", "x"))
    seq, fsdp = ("zh", "y", "c"), ("zl", "x")
    return jax.shard_map(
        per_device,
        mesh=fine,
        in_specs=(
            P(seq, None),
            P(seq, None),
            P(seq),
            P(seq, fsdp, None),
            P(seq, fsdp),
            P(seq, fsdp),
        ),
        out_specs=(P(seq, fsdp),) * 4,
        check_vma=False,
    )
```

time: 585 us -> 267 us (0.46)
  waiting for transfers between devices: 273 us -> 97.7 us
  local copies, waits for them, and re-layouts: 104 us -> 9.2 us
  blocking collectives: 88 us -> 0 us
  Pallas kernels: 0 us -> 62 us
  starting transfers between devices: 45.7 us -> 86 us
  matrix products: 33.5 us -> 0 us
  other arithmetic: 24.6 us -> 9.44 us
  between operations: 14 us -> 0.94 us
    reduce_scatter x2 -> x0, waiting for transfers between devices: 169 us -> none  [the longest x1 94.2 us: per_device(): lax.psum_scatter(grad_qkv_local, 'seq', scatter_dimension=0, tiled=True)]
    ppermute x0 -> x30, waiting for transfers between devices: none -> 97.7 us  [the longest x27 81.4 us: shift(): return lax.ppermute(value, axis, [(i, (i + k) % size) for i in range(size)])]
    all_gather x1 -> x0, blocking collectives: 88 us -> none  [per_device(): lax.all_gather(out_weight, 'seq', axis=0, tiled=True)]
    ppermute x0 -> x30, starting transfers between devices: none -> 62.8 us  [the longest x27 51.9 us: shift(): return lax.ppermute(value, axis, [(i, (i + k) % size) for i in range(size)])]
    pallas_call x0 -> x5, Pallas kernels: none -> 62 us  [the longest x1 27.6 us: layer(): pl.pallas_call(layer_kernel, out_shape=(half,) * 8 + (quarter,) * 4, in_s...]
    all_to_all x4 -> x3, waiting for transfers between devices: 52.9 us -> 0.01 us  [the longest x1 0.01 us: per_device(): lax.all_to_all(summed.astype(BF).reshape(8, 40, 640), ('zh', 'zl'), split...]
    gather x8 -> x0, local copies, waits for them, and re-layouts: 51.8 us -> none  [the longest x2 10.6 us: restore(): outgoing = window_rows[recv_slot]]
    unnamed x7 -> x0, waiting for transfers between devices: 51.3 us -> none
  transfers between devices with their start and end apart: 9 -> 33, of which waited for: 5 -> 11; matrix products, arithmetic and copies ran while one was open for 17% -> 4% of each run, Pallas kernels for 0% -> 11%
where the time goes in v1:
time: 267 us; the launch traced here: 265 us
  waiting for transfers between devices  97.7 us (37%)
  starting transfers between devices  86 us (32%)
  Pallas kernels  62 us (23%)
  other arithmetic  9.44 us (4%)
  local copies, waits for them, and re-layouts  9.2 us (3%)
    ppermute x27, waiting for transfers between devices, shift(): return lax.ppermute(value, axis, [(i, (i + k) % size) for i in range(size)])  81.4 us
    ppermute x27, starting transfers between devices, shift(): return lax.ppermute(value, axis, [(i, (i + k) % size) for i in range(size)])  51.9 us
    pallas_call x1, Pallas kernels, layer(): pl.pallas_call(layer_kernel, out_shape=(half,) * 8 + (quarter,) * 4, in_s...  27.6 us
    pallas_call x1, Pallas kernels, pick(): pl.pallas_call(pick_kernel, out_shape=jax.ShapeDtypeStruct((16, 2, 8, D),...  21.9 us
    ppermute x3, waiting for transfers between devices, swap(): return lax.ppermute(value, ('c', 'zl'), [(0, 0), (1, 2), (2, 1), (3, 3)])  16.3 us
    ppermute x3, starting transfers between devices, swap(): return lax.ppermute(value, ('c', 'zl'), [(0, 0), (1, 2), (2, 1), (3, 3)])  10.9 us
    all_to_all x1, starting transfers between devices, per_device(): lax.all_to_all(sent, ('zh', 'y'), split_axis=0, concat_axis=0, tiled=True)  10.5 us
    all_to_all x1, starting transfers between devices, per_device(): lax.all_to_all(message, ('zh', 'y', 'zl'), split_axis=0, concat_axis=0, t...  9.12 us
  transfers between devices with their start and end apart: 33, of which 11 were waited for; matrix products, arithmetic and copies ran while one was open for 4% of the time, Pallas kernels for 11%

profile of v1, /device:TPU:1, one launch (start us, length us, event | category | flops | bytes accessed | tf_op | source)
XLA Modules:
  0.0 265.3 jit_solution(5009258191099407833)
XLA Ops:
  0.6 0.9 pad_maximum_fusion
  1.5 4.9 %collective-permute-start.7 = (bf16[40,640]{1,0:T(8,128)(2,1)S(1)}, bf16[40,640]{1,0:T(8,128)(2,1)S(1)}, u32[]{:S(2)}, u32[]{:S(2)}) collective-permute-start(bf16[40,640]{1,0:T(8,128)(2,1)S(1)} %pad_maximum_fusion), channel_id=1, source_target_pairs={{0,0},{4,8},{8,4},{12,12},{1,1},{5,9},{9,5},{13,13},{2,2},{6,10},{... | collective-permute-start | bytes 153608 | tf_op jit(solution)/shard_map/ppermute | solution.py:337
  6.4 1.2 convert_element_type.48
  7.7 1.9 collective-permute-start.18
  9.6 0.7 slice.28
  10.4 0.1 slice_reduce_fusion
  10.5 0.2 select_reduce_fusion
  10.7 0.6 pad_add_fusion.2.idx_ref
  11.3 21.9 %pick_rows.1 = bf16[16,2,8,1280]{3,2,1,0:T(8,128)(2,1)} custom-call(s32[17]{0:T(128)} %pad_add_fusion.2.idx_ref, bf16[4,32,8,1280]{3,2,1,0:T(8,128)(2,1)} %bitcast.36, bf16[4,32,8,1280]{3,2,1,0:T(8,128)(2,1)} %bitcast.37), custom_call_target="tpu_custom_call" | custom-call | bytes 2097152 | tf_op jit(solution)/shard_map/pick_rows/pallas_call | solution.py:60
  33.2 10.5 %all-to-all-start = ((bf16[16,2,8,1280]{3,2,1,0:T(8,128)(2,1)}), bf16[16,2,8,1280]{3,2,1,0:T(8,128)(2,1)S(1)}, u32[]{:S(2)}, u32[]{:S(2)}) async-start(bf16[16,2,8,1280]{3,2,1,0:T(8,128)(2,1)} %pick_rows.1), calls=%async_computation | async-start | bytes 1310720 | tf_op jit(solution)/shard_map/all_to_all | solution.py:348
  43.7 0.1 collective-permute-start.14
  43.8 3.6 %collective-permute-start.13 = (bf16[40,640]{1,0:T(8,128)(2,1)S(1)}, bf16[40,640]{1,0:T(8,128)(2,1)S(1)}, u32[]{:S(2)}, u32[]{:S(2)}) collective-permute-start(bf16[40,640]{1,0:T(8,128)(2,1)S(1)} %collective-permute-done.7), channel_id=1, source_target_pairs={{0,192},{4,196},{64,0},{68,4},{128,64},{132,68},{192,128},{196,132... | collective-permute-start | bytes 153608 | tf_op jit(solution)/shard_map/ppermute | solution.py:333
  47.4 2.3 collective-permute-start.12
  49.6 1.0 collective-permute-start.8
  50.6 8.4 %collective-permute-done.8 = bf16[40,640]{1,0:T(8,128)(2,1)S(1)} collective-permute-done((bf16[40,640]{1,0:T(8,128)(2,1)S(1)}, bf16[40,640]{1,0:T(8,128)(2,1)S(1)}, u32[]{:S(2)}, u32[]{:S(2)}) %collective-permute-start.8) | collective-permute-done | bytes 51232 | tf_op jit(solution)/shard_map/ppermute | solution.py:333
  59.1 5.1 %collective-permute-done.9 = bf16[40,640]{1,0:T(8,128)(2,1)S(1)} collective-permute-done((bf16[40,640]{1,0:T(8,128)(2,1)S(1)}, bf16[40,640]{1,0:T(8,128)(2,1)S(1)}, u32[]{:S(2)}, u32[]{:S(2)}) %collective-permute-start.9) | collective-permute-done | bytes 51232 | tf_op jit(solution)/shard_map/ppermute | solution.py:333
  64.1 7.3 %collective-permute-done.10 = bf16[40,640]{1,0:T(8,128)(2,1)S(1)} collective-permute-done((bf16[40,640]{1,0:T(8,128)(2,1)S(1)}, bf16[40,640]{1,0:T(8,128)(2,1)S(1)}, u32[]{:S(2)}, u32[]{:S(2)}) %collective-permute-start.10) | collective-permute-done | bytes 51232 | tf_op jit(solution)/shard_map/ppermute | solution.py:333
  71.4 6.9 %collective-permute-done.11 = bf16[40,640]{1,0:T(8,128)(2,1)S(1)} collective-permute-done((bf16[40,640]{1,0:T(8,128)(2,1)S(1)}, bf16[40,640]{1,0:T(8,128)(2,1)S(1)}, u32[]{:S(2)}, u32[]{:S(2)}) %collective-permute-start.11) | collective-permute-done | bytes 51232 | tf_op jit(solution)/shard_map/ppermute | solution.py:333
  78.4 2.6 collective-permute-start.2
  80.9 0.5 collective-permute-start.1
  81.4 0.6 collective-permute-start
  82.1 2.6 collective-permute-start.17
  84.7 0.6 collective-permute-start.16
  85.3 7.7 %collective-permute-done.17.w3 = bf16[8,40,640]{2,1,0:T(8,128)(2,1)S(1)} collective-permute-done((bf16[8,40,640]{2,1,0:T(8,128)(2,1)S(1)}, bf16[8,40,640]{2,1,0:T(8,128)(2,1)S(1)}, u32[]{:S(2)}, u32[]{:S(2)}) %collective-permute-start.17) | collective-permute-done | bytes 409632 | tf_op jit(solution)/shard_map/ppermute | solution.py:333
  93.0 10.2 %collective-permute-start.3 = (bf16[16,2,8,1280]{3,2,1,0:T(8,128)(2,1)S(1)}, bf16[16,2,8,1280]{3,2,1,0:T(8,128)(2,1)}, u32[]{:S(2)}, u32[]{:S(2)}) collective-permute-start(bf16[16,2,8,1280]{3,2,1,0:T(8,128)(2,1)S(1)} %all-to-all-done.refs_0_), channel_id=1, source_target_pairs={{0,8},{8,0},{1,9},{9,1},{2,10},{10,2},{3,11},{11,3},{4,12},{12,4},... | collective-permute-start | bytes 1966088 | tf_op jit(solution)/shard_map/ppermute | solution.py:333
  103.2 6.8 %collective-permute-start.6 = (bf16[16,2,8,1280]{3,2,1,0:T(8,128)(2,1)}, bf16[16,2,8,1280]{3,2,1,0:T(8,128)(2,1)}, u32[]{:S(2)}, u32[]{:S(2)}) collective-permute-start(bf16[16,2,8,1280]{3,2,1,0:T(8,128)(2,1)} %collective-permute-done.2.refs_3_), channel_id=1, source_target_pairs={{0,8},{8,0},{1,9},{9,1},{2,10},{10,2},{3,11},{11,3},{4,12},{12,4},... | collective-permute-start | bytes 1966088 | tf_op jit(solution)/shard_map/ppermute | solution.py:333
  110.0 3.3 %collective-permute-done.refs_1_ = bf16[16,2,8,1280]{3,2,1,0:T(8,128)(2,1)} collective-permute-done((bf16[16,2,8,1280]{3,2,1,0:T(8,128)(2,1)S(1)}, bf16[16,2,8,1280]{3,2,1,0:T(8,128)(2,1)}, u32[]{:S(2)}, u32[]{:S(2)}) %collective-permute-start) | collective-permute-done | bytes 655392 | tf_op jit(solution)/shard_map/ppermute | solution.py:333
  113.2 0.5 collective-permute-start.4
  113.8 1.5 collective-permute-start.15
  115.3 0.6 pad_add_fusion.1.idx_ref
  115.9 0.3 reshape.78
  116.4 1.0 fusion.2.refs_12_
  117.4 8.9 %collective-permute-done.15.w1 = bf16[8,40,640]{2,1,0:T(8,128)(2,1)S(1)} collective-permute-done((bf16[8,40,640]{2,1,0:T(8,128)(2,1)S(1)}, bf16[8,40,640]{2,1,0:T(8,128)(2,1)S(1)}, u32[]{:S(2)}, u32[]{:S(2)}) %collective-permute-start.15) | collective-permute-done | bytes 409632 | tf_op jit(solution)/shard_map/ppermute | solution.py:333
  126.3 6.0 %arrange_weights.1 = (bf16[1280,768]{1,0:T(8,128)(2,1)S(1)}, bf16[1280,256]{1,0:T(8,128)(2,1)S(1)}, bf16[4,512,256]{2,1,0:T(8,128)(2,1)S(1)}, bf16[4,384,768]{2,1,0:T(8,128)(2,1)S(1)}) custom-call(s32[2]{0:T(128)S(1)} %pad_add_fusion.3.idx_ref, bf16[8,40,640]{2,1,0:T(8,128)(2,1)S(1)} %bitcast_dynamic-update-slice_fusion.w0, ...), custom_call_target="tpu_custom_call" | custom-call | flops 1677721600 | bytes 8388608 | tf_op jit(solution)/shard_map/arrange_weights/pallas_call | solution.py:114
  132.3 1.4 copy-done.1
  133.7 1.3 copy-done.2
  135.0 1.0 copy-done.3
  136.0 0.8 copy-done.4
  136.9 27.6 %layer.1 = (bf16[16,32,640]{2,1,0:T(8,128)(2,1)}, bf16[16,32,640]{2,1,0:T(8,128)(2,1)}, bf16[16,32,640]{2,1,0:T(8,128)(2,1)}, bf16[16,32,640]{2,1,0:T(8,128)(2,1...) custom-call(s32[3]{0:T(128)} %pad_add_fusion.1.idx_ref, ...), custom_call_target="tpu_custom_call" | custom-call | flops 12884901888 | bytes 25165824 | tf_op jit(solution)/shard_map/layer/pallas_call | solution.py:250
  164.5 0.2 collective-permute-start.26
  164.7 2.4 collective-permute-start.27
  167.1 1.2 collective-permute-start.28
  168.3 1.6 collective-permute-start.20
  169.9 6.5 %collective-permute-done.26 = bf16[4,80,640]{2,1,0:T(8,128)(2,1)S(1)} collective-permute-done((bf16[4,80,640]{2,1,0:T(8,128)(2,1)}, bf16[4,80,640]{2,1,0:T(8,128)(2,1)S(1)}, u32[]{:S(2)}, u32[]{:S(2)}) %collective-permute-start.26) | collective-permute-done | bytes 409632 | tf_op jit(solution)/shard_map/ppermute | solution.py:333
  176.4 10.3 %collective-permute-start.19 = (bf16[16,32,640]{2,1,0:T(8,128)(2,1)}, bf16[16,32,640]{2,1,0:T(8,128)(2,1)S(1)}, u32[]{:S(2)}, u32[]{:S(2)}) collective-permute-start(bf16[16,32,640]{2,1,0:T(8,128)(2,1)} %get-tuple-element.27), channel_id=1, source_target_pairs={{0,8},{8,0},{1,9},{9,1},{2,10},{10,2},{3,11},{11,3},{4,12},{12,4},... | collective-permute-start | bytes 1966088 | tf_op jit(solution)/shard_map/ppermute | solution.py:333
  186.7 2.1 add_convert_fusion.3
  188.7 3.6 %all-to-all-start.2 = ((bf16[8,40,640]{2,1,0:T(8,128)(2,1)}), bf16[8,40,640]{2,1,0:T(8,128)(2,1)S(1)}, u32[]{:S(2)}, u32[]{:S(2)}) async-start(bf16[8,40,640]{2,1,0:T(8,128)(2,1)} %bitcast.21), calls=%async_computation.2 | async-start | bytes 819200 | tf_op jit(solution)/shard_map/all_to_all | solution.py:381
  192.3 1.2 add_convert_fusion.2
  193.6 0.6 collective-permute-start.21
  194.2 0.2 add_convert_fusion.1
  194.4 0.5 collective-permute-start.23
  194.9 1.2 add_convert_fusion
  196.1 2.4 collective-permute-start.25
  198.5 12.4 %collective-permute-done.21.p2 = bf16[16,32,640]{2,1,0:T(8,128)(2,1)S(1)} collective-permute-done((bf16[16,32,640]{2,1,0:T(8,128)(2,1)S(1)}, bf16[16,32,640]{2,1,0:T(8,128)(2,1)S(1)}, u32[]{:S(2)}, u32[]{:S(2)}) %collective-permute-start.21) | collective-permute-done | bytes 655392 | tf_op jit(solution)/shard_map/ppermute | solution.py:333
  210.9 15.0 %collective-permute-done.23.p3 = bf16[16,32,640]{2,1,0:T(8,128)(2,1)S(1)} collective-permute-done((bf16[16,32,640]{2,1,0:T(8,128)(2,1)S(1)}, bf16[16,32,640]{2,1,0:T(8,128)(2,1)S(1)}, u32[]{:S(2)}, u32[]{:S(2)}) %collective-permute-start.23) | collective-permute-done | bytes 655392 | tf_op jit(solution)/shard_map/ppermute | solution.py:333
  225.9 1.4 total.1
  227.3 9.1 %all-to-all-start.1 = ((bf16[32,32,384]{2,1,0:T(8,128)(2,1)}), bf16[32,32,384]{2,1,0:T(8,128)(2,1)S(1)}, u32[]{:S(2)}, u32[]{:S(2)}) async-start(bf16[32,32,384]{2,1,0:T(8,128)(2,1)} %bitcast.18), calls=%async_computation.1 | async-start | bytes 1572864 | tf_op jit(solution)/shard_map/all_to_all | solution.py:375
  236.5 4.1 %collective-permute-start.29 = (f32[40,640]{1,0:T(8,128)S(1)}, f32[40,640]{1,0:T(8,128)S(1)}, u32[]{:S(2)}, u32[]{:S(2)}) collective-permute-start(f32[40,640]{1,0:T(8,128)S(1)} %broadcast_multiply_fusion), channel_id=1, source_target_pairs={{0,0},{4,8},{8,4},{12,12},{1,1},{5,9},{9,5},{13,13},{2,2},{6,10},{... | collective-permute-start | bytes 307208 | tf_op jit(solution)/shard_map/ppermute | solution.py:337
  240.7 16.3 %collective-permute-done.29 = f32[40,640]{1,0:T(8,128)S(1)} collective-permute-done((f32[40,640]{1,0:T(8,128)S(1)}, f32[40,640]{1,0:T(8,128)S(1)}, u32[]{:S(2)}, u32[]{:S(2)}) %collective-permute-start.29) | collective-permute-done | bytes 102432 | tf_op jit(solution)/shard_map/ppermute | solution.py:337
  256.9 0.7 slice.39
  257.6 0.6 slice.38
  258.3 5.1 %restore.1 = (bf16[4,256,160]{2,1,0:T(8,128)(2,1)S(1)}, bf16[4,256,160]{2,1,0:T(8,128)(2,1)S(1)}) custom-call(s32[33]{0:T(128)S(1)} %pad_add_fusion.idx_ref, bf16[32,32,384]{2,1,0:T(8,128)(2,1)S(1)} %all-to-all-done.1.got_ref), custom_call_target="tpu_custom_call" | custom-call | bytes 2097152 | tf_op jit(solution)/shard_map/restore/pallas_call | solution.py:320
  263.4 1.0 copy.22
  264.4 0.9 copy.23
  (59 shorter events, 0.6 us)
Async XLA Ops:
  1.5 42.2 %collective-permute-start.7 = (bf16[40,640]{1,0:T(8,128)(2,1)S(1)}, bf16[40,640]{1,0:T(8,128)(2,1)S(1)}, u32[]{:S(2)}, u32[]{:S(2)}) collective-permute-start(bf16[40,640]{1,0:T(8,128)(2,1)S(1)} %pad_maximum_fusion), channel_id=1, source_target_pairs={{0,0},{4,8},{8,4},{12,12},{1,1},{5,9},{9,5},{13,13},{2,2},{6,10},{... | collective-permute-start | bytes 153608 | tf_op jit(solution)/shard_map/ppermute | solution.py:337
  7.7 77.0 %collective-permute-start.18 = (bf16[16,2,4096]{2,1,0:T(2,128)(2,1)S(1)}, bf16[16,2,4096]{2,1,0:T(2,128)(2,1)S(1)}, u32[]{:S(2)}, u32[]{:S(2)}) collective-permute-start(bf16[16,2,4096]{2,1,0:T(2,128)(2,1)S(1)} %convert_element_type.48), channel_id=1, source_target_pairs={{0,0},{4,8},{8,4},{12,12},{1,1},{5,9},{9,5},{13,13},{2,2},{6,10},{... | collective-permute-start | bytes 786440 | tf_op jit(solution)/shard_map/ppermute | solution.py:337
  33.2 45.1 %all-to-all-start = ((bf16[16,2,8,1280]{3,2,1,0:T(8,128)(2,1)}), bf16[16,2,8,1280]{3,2,1,0:T(8,128)(2,1)S(1)}, u32[]{:S(2)}, u32[]{:S(2)}) async-start(bf16[16,2,8,1280]{3,2,1,0:T(8,128)(2,1)} %pick_rows.1), calls=%async_computation | async-start | bytes 1310720 | tf_op jit(solution)/shard_map/all_to_all | solution.py:348
  43.7 38.3 %collective-permute-start.14 = (bf16[40,640]{1,0:T(8,128)(2,1)S(1)}, bf16[40,640]{1,0:T(8,128)(2,1)S(1)}, u32[]{:S(2)}, u32[]{:S(2)}) collective-permute-start(bf16[40,640]{1,0:T(8,128)(2,1)S(1)} %collective-permute-done.7), channel_id=1, source_target_pairs={{0,196},{4,0},{64,4},{68,64},{128,68},{132,128},{192,132},{196,192... | collective-permute-start | bytes 153608 | tf_op jit(solution)/shard_map/ppermute | solution.py:333
  43.8 37.6 %collective-permute-start.13 = (bf16[40,640]{1,0:T(8,128)(2,1)S(1)}, bf16[40,640]{1,0:T(8,128)(2,1)S(1)}, u32[]{:S(2)}, u32[]{:S(2)}) collective-permute-start(bf16[40,640]{1,0:T(8,128)(2,1)S(1)} %collective-permute-done.7), channel_id=1, source_target_pairs={{0,192},{4,196},{64,0},{68,4},{128,64},{132,68},{192,128},{196,132... | collective-permute-start | bytes 153608 | tf_op jit(solution)/shard_map/ppermute | solution.py:333
  47.4 30.9 %collective-permute-start.12 = (bf16[40,640]{1,0:T(8,128)(2,1)S(1)}, bf16[40,640]{1,0:T(8,128)(2,1)S(1)}, u32[]{:S(2)}, u32[]{:S(2)}) collective-permute-start(bf16[40,640]{1,0:T(8,128)(2,1)S(1)} %collective-permute-done.7), channel_id=1, source_target_pairs={{0,132},{4,192},{64,196},{68,0},{128,4},{132,64},{192,68},{196,128... | collective-permute-start | bytes 153608 | tf_op jit(solution)/shard_map/ppermute | solution.py:333
  49.6 9.4 %collective-permute-start.8 = (bf16[40,640]{1,0:T(8,128)(2,1)S(1)}, bf16[40,640]{1,0:T(8,128)(2,1)S(1)}, u32[]{:S(2)}, u32[]{:S(2)}) collective-permute-start(bf16[40,640]{1,0:T(8,128)(2,1)S(1)} %collective-permute-done.7), channel_id=1, source_target_pairs={{0,4},{4,64},{64,68},{68,128},{128,132},{132,192},{192,196},{196,0... | collective-permute-start | bytes 153608 | tf_op jit(solution)/shard_map/ppermute | solution.py:333
  59.0 5.1 %collective-permute-start.9 = (bf16[40,640]{1,0:T(8,128)(2,1)S(1)}, bf16[40,640]{1,0:T(8,128)(2,1)S(1)}, u32[]{:S(2)}, u32[]{:S(2)}) collective-permute-start(bf16[40,640]{1,0:T(8,128)(2,1)S(1)} %collective-permute-done.7), channel_id=1, source_target_pairs={{0,64},{4,68},{64,128},{68,132},{128,192},{132,196},{192,0},{196,4... | collective-permute-start | bytes 153608 | tf_op jit(solution)/shard_map/ppermute | solution.py:333
  64.1 7.3 %collective-permute-start.10 = (bf16[40,640]{1,0:T(8,128)(2,1)S(1)}, bf16[40,640]{1,0:T(8,128)(2,1)S(1)}, u32[]{:S(2)}, u32[]{:S(2)}) collective-permute-start(bf16[40,640]{1,0:T(8,128)(2,1)S(1)} %collective-permute-done.7), channel_id=1, source_target_pairs={{0,68},{4,128},{64,132},{68,192},{128,196},{132,0},{192,4},{196,64... | collective-permute-start | bytes 153608 | tf_op jit(solution)/shard_map/ppermute | solution.py:333
  71.4 6.9 %collective-permute-start.11 = (bf16[40,640]{1,0:T(8,128)(2,1)S(1)}, bf16[40,640]{1,0:T(8,128)(2,1)S(1)}, u32[]{:S(2)}, u32[]{:S(2)}) collective-permute-start(bf16[40,640]{1,0:T(8,128)(2,1)S(1)} %collective-permute-done.7), channel_id=1, source_target_pairs={{0,128},{4,132},{64,192},{68,196},{128,0},{132,4},{192,64},{196,68... | collective-permute-start | bytes 153608 | tf_op jit(solution)/shard_map/ppermute | solution.py:333
  78.4 38.0 %copy-start.5 = (bf16[16,2,8,1280]{3,2,1,0:T(8,128)(2,1)}, bf16[16,2,8,1280]{3,2,1,0:T(8,128)(2,1)S(1)}, u32[]{:S(2)}) copy-start(bf16[16,2,8,1280]{3,2,1,0:T(8,128)(2,1)S(1)} %all-to-all-done.refs_0_) | copy-start | bytes 1966084
  78.4 24.8 %collective-permute-start.2 = (bf16[16,2,8,1280]{3,2,1,0:T(8,128)(2,1)S(1)}, bf16[16,2,8,1280]{3,2,1,0:T(8,128)(2,1)}, u32[]{:S(2)}, u32[]{:S(2)}) collective-permute-start(bf16[16,2,8,1280]{3,2,1,0:T(8,128)(2,1)S(1)} %all-to-all-done.refs_0_), channel_id=1, source_target_pairs={{0,3},{1,0},{2,1},{3,2},{4,7},{5,4},{6,5},{7,6},{8,11},{9,8},{10,9... | collective-permute-start | bytes 1966088 | tf_op jit(solution)/shard_map/ppermute | solution.py:333
  80.9 29.0 %collective-permute-start.1 = (bf16[16,2,8,1280]{3,2,1,0:T(8,128)(2,1)S(1)}, bf16[16,2,8,1280]{3,2,1,0:T(8,128)(2,1)}, u32[]{:S(2)}, u32[]{:S(2)}) collective-permute-start(bf16[16,2,8,1280]{3,2,1,0:T(8,128)(2,1)S(1)} %all-to-all-done.refs_0_), channel_id=1, source_target_pairs={{0,2},{1,3},{2,0},{3,1},{4,6},{5,7},{6,4},{7,5},{8,10},{9,11},{10,... | collective-permute-start | bytes 1966088 | tf_op jit(solution)/shard_map/ppermute | solution.py:333
  81.4 31.8 %collective-permute-start = (bf16[16,2,8,1280]{3,2,1,0:T(8,128)(2,1)S(1)}, bf16[16,2,8,1280]{3,2,1,0:T(8,128)(2,1)}, u32[]{:S(2)}, u32[]{:S(2)}) collective-permute-start(bf16[16,2,8,1280]{3,2,1,0:T(8,128)(2,1)S(1)} %all-to-all-done.refs_0_), channel_id=1, source_target_pairs={{0,1},{1,2},{2,3},{3,0},{4,5},{5,6},{6,7},{7,4},{8,9},{9,10},{10,1... | collective-permute-start | bytes 1966088 | tf_op jit(solution)/shard_map/ppermute | solution.py:333
  82.1 10.9 %collective-permute-start.17 = (bf16[8,40,640]{2,1,0:T(8,128)(2,1)S(1)}, bf16[8,40,640]{2,1,0:T(8,128)(2,1)S(1)}, u32[]{:S(2)}, u32[]{:S(2)}) collective-permute-start(bf16[8,40,640]{2,1,0:T(8,128)(2,1)S(1)} %bitcast_dynamic-update-slice_fusion.w0), channel_id=1, source_target_pairs={{0,48},{16,0},{32,16},{48,32},{1,49},{17,1},{33,17},{49,33},{2,50}... | collective-permute-start | bytes 1228808 | tf_op jit(solution)/shard_map/ppermute | solution.py:333
  84.7 29.1 %collective-permute-start.16 = (bf16[8,40,640]{2,1,0:T(8,128)(2,1)S(1)}, bf16[8,40,640]{2,1,0:T(8,128)(2,1)S(1)}, u32[]{:S(2)}, u32[]{:S(2)}) collective-permute-start(bf16[8,40,640]{2,1,0:T(8,128)(2,1)S(1)} %bitcast_dynamic-update-slice_fusion.w0), channel_id=1, source_target_pairs={{0,32},{16,48},{32,0},{48,16},{1,33},{17,49},{33,1},{49,17},{2,34}... | collective-permute-start | bytes 1228808 | tf_op jit(solution)/shard_map/ppermute | solution.py:333
  93.0 43.9 %collective-permute-start.3 = (bf16[16,2,8,1280]{3,2,1,0:T(8,128)(2,1)S(1)}, bf16[16,2,8,1280]{3,2,1,0:T(8,128)(2,1)}, u32[]{:S(2)}, u32[]{:S(2)}) collective-permute-start(bf16[16,2,8,1280]{3,2,1,0:T(8,128)(2,1)S(1)} %all-to-all-done.refs_0_), channel_id=1, source_target_pairs={{0,8},{8,0},{1,9},{9,1},{2,10},{10,2},{3,11},{11,3},{4,12},{12,4},... | collective-permute-start | bytes 1966088 | tf_op jit(solution)/shard_map/ppermute | solution.py:333
  103.2 33.7 %collective-permute-start.6 = (bf16[16,2,8,1280]{3,2,1,0:T(8,128)(2,1)}, bf16[16,2,8,1280]{3,2,1,0:T(8,128)(2,1)}, u32[]{:S(2)}, u32[]{:S(2)}) collective-permute-start(bf16[16,2,8,1280]{3,2,1,0:T(8,128)(2,1)} %collective-permute-done.2.refs_3_), channel_id=1, source_target_pairs={{0,8},{8,0},{1,9},{9,1},{2,10},{10,2},{3,11},{11,3},{4,12},{12,4},... | collective-permute-start | bytes 1966088 | tf_op jit(solution)/shard_map/ppermute | solution.py:333
  109.9 26.9 %collective-permute-start.5 = (bf16[16,2,8,1280]{3,2,1,0:T(8,128)(2,1)}, bf16[16,2,8,1280]{3,2,1,0:T(8,128)(2,1)}, u32[]{:S(2)}, u32[]{:S(2)}) collective-permute-start(bf16[16,2,8,1280]{3,2,1,0:T(8,128)(2,1)} %collective-permute-done.1.refs_2_), channel_id=1, source_target_pairs={{0,8},{8,0},{1,9},{9,1},{2,10},{10,2},{3,11},{11,3},{4,12},{12,4},... | collective-permute-start | bytes 1966088 | tf_op jit(solution)/shard_map/ppermute | solution.py:333
  113.2 23.7 %collective-permute-start.4 = (bf16[16,2,8,1280]{3,2,1,0:T(8,128)(2,1)}, bf16[16,2,8,1280]{3,2,1,0:T(8,128)(2,1)}, u32[]{:S(2)}, u32[]{:S(2)}) collective-permute-start(bf16[16,2,8,1280]{3,2,1,0:T(8,128)(2,1)} %collective-permute-done.refs_1_), channel_id=1, source_target_pairs={{0,8},{8,0},{1,9},{9,1},{2,10},{10,2},{3,11},{11,3},{4,12},{12,4},... | collective-permute-start | bytes 1966088 | tf_op jit(solution)/shard_map/ppermute | solution.py:333
  113.8 12.5 %collective-permute-start.15 = (bf16[8,40,640]{2,1,0:T(8,128)(2,1)S(1)}, bf16[8,40,640]{2,1,0:T(8,128)(2,1)S(1)}, u32[]{:S(2)}, u32[]{:S(2)}) collective-permute-start(bf16[8,40,640]{2,1,0:T(8,128)(2,1)S(1)} %bitcast_dynamic-update-slice_fusion.w0), channel_id=1, source_target_pairs={{0,16},{16,32},{32,48},{48,0},{1,17},{17,33},{33,49},{49,1},{2,18}... | collective-permute-start | bytes 1228808 | tf_op jit(solution)/shard_map/ppermute | solution.py:333
  132.3 1.4 copy-start.1
  133.7 1.3 copy-start.2
  135.0 1.0 copy-start.3
  136.0 0.8 copy-start.4
  164.5 11.9 %collective-permute-start.26 = (bf16[4,80,640]{2,1,0:T(8,128)(2,1)}, bf16[4,80,640]{2,1,0:T(8,128)(2,1)S(1)}, u32[]{:S(2)}, u32[]{:S(2)}) collective-permute-start(bf16[4,80,640]{2,1,0:T(8,128)(2,1)} %get-tuple-element.37), channel_id=1, source_target_pairs={{0,16},{16,32},{32,48},{48,0},{1,17},{17,33},{33,49},{49,1},{2,18}... | collective-permute-start | bytes 1228808 | tf_op jit(solution)/shard_map/ppermute | solution.py:333
  164.7 22.0 %collective-permute-start.27 = (bf16[4,80,640]{2,1,0:T(8,128)(2,1)}, bf16[4,80,640]{2,1,0:T(8,128)(2,1)S(1)}, u32[]{:S(2)}, u32[]{:S(2)}) collective-permute-start(bf16[4,80,640]{2,1,0:T(8,128)(2,1)} %get-tuple-element.38), channel_id=1, source_target_pairs={{0,32},{16,48},{32,0},{48,16},{1,33},{17,49},{33,1},{49,17},{2,34}... | collective-permute-start | bytes 1228808 | tf_op jit(solution)/shard_map/ppermute | solution.py:333
  167.1 19.6 %collective-permute-start.28 = (bf16[4,80,640]{2,1,0:T(8,128)(2,1)}, bf16[4,80,640]{2,1,0:T(8,128)(2,1)S(1)}, u32[]{:S(2)}, u32[]{:S(2)}) collective-permute-start(bf16[4,80,640]{2,1,0:T(8,128)(2,1)} %get-tuple-element.39), channel_id=1, source_target_pairs={{0,48},{16,0},{32,16},{48,32},{1,49},{17,1},{33,17},{49,33},{2,50}... | collective-permute-start | bytes 1228808 | tf_op jit(solution)/shard_map/ppermute | solution.py:333
  168.3 24.1 %collective-permute-start.20 = (bf16[16,32,640]{2,1,0:T(8,128)(2,1)}, bf16[16,32,640]{2,1,0:T(8,128)(2,1)}, u32[]{:S(2)}, u32[]{:S(2)}) collective-permute-start(bf16[16,32,640]{2,1,0:T(8,128)(2,1)} %get-tuple-element.29), channel_id=1, source_target_pairs={{0,8},{8,0},{1,9},{9,1},{2,10},{10,2},{3,11},{11,3},{4,12},{12,4},... | collective-permute-start | bytes 1966088 | tf_op jit(solution)/shard_map/ppermute | solution.py:333
  169.9 24.3 %collective-permute-start.22 = (bf16[16,32,640]{2,1,0:T(8,128)(2,1)}, bf16[16,32,640]{2,1,0:T(8,128)(2,1)S(1)}, u32[]{:S(2)}, u32[]{:S(2)}) collective-permute-start(bf16[16,32,640]{2,1,0:T(8,128)(2,1)} %get-tuple-element.31), channel_id=1, source_target_pairs={{0,8},{8,0},{1,9},{9,1},{2,10},{10,2},{3,11},{11,3},{4,12},{12,4},... | collective-permute-start | bytes 1966088 | tf_op jit(solution)/shard_map/ppermute | solution.py:333
  176.4 22.1 %collective-permute-start.19 = (bf16[16,32,640]{2,1,0:T(8,128)(2,1)}, bf16[16,32,640]{2,1,0:T(8,128)(2,1)S(1)}, u32[]{:S(2)}, u32[]{:S(2)}) collective-permute-start(bf16[16,32,640]{2,1,0:T(8,128)(2,1)} %get-tuple-element.27), channel_id=1, source_target_pairs={{0,8},{8,0},{1,9},{9,1},{2,10},{10,2},{3,11},{11,3},{4,12},{12,4},... | collective-permute-start | bytes 1966088 | tf_op jit(solution)/shard_map/ppermute | solution.py:333
  186.6 8.2 %collective-permute-start.24 = (bf16[16,32,640]{2,1,0:T(8,128)(2,1)}, bf16[16,32,640]{2,1,0:T(8,128)(2,1)}, u32[]{:S(2)}, u32[]{:S(2)}) collective-permute-start(bf16[16,32,640]{2,1,0:T(8,128)(2,1)} %get-tuple-element.33), channel_id=1, source_target_pairs={{0,8},{8,0},{1,9},{9,1},{2,10},{10,2},{3,11},{11,3},{4,12},{12,4},... | collective-permute-start | bytes 1966088 | tf_op jit(solution)/shard_map/ppermute | solution.py:333
  186.7 5.7 %copy-start.8 = (bf16[16,32,640]{2,1,0:T(8,128)(2,1)S(1)}, bf16[16,32,640]{2,1,0:T(8,128)(2,1)}, u32[]{:S(2)}) copy-start(bf16[16,32,640]{2,1,0:T(8,128)(2,1)} %get-tuple-element.28) | copy-start | bytes 1966084
  188.7 5.5 %copy-start.7 = (bf16[16,32,640]{2,1,0:T(8,128)(2,1)S(1)}, bf16[16,32,640]{2,1,0:T(8,128)(2,1)}, u32[]{:S(2)}) copy-start(bf16[16,32,640]{2,1,0:T(8,128)(2,1)} %get-tuple-element.30) | copy-start | bytes 1966084
  188.7 38.6 %all-to-all-start.2 = ((bf16[8,40,640]{2,1,0:T(8,128)(2,1)}), bf16[8,40,640]{2,1,0:T(8,128)(2,1)S(1)}, u32[]{:S(2)}, u32[]{:S(2)}) async-start(bf16[8,40,640]{2,1,0:T(8,128)(2,1)} %bitcast.21), calls=%async_computation.2 | async-start | bytes 819200 | tf_op jit(solution)/shard_map/all_to_all | solution.py:381
  193.6 1.3 copy-start.6
  193.6 17.3 %collective-permute-start.21 = (bf16[16,32,640]{2,1,0:T(8,128)(2,1)S(1)}, bf16[16,32,640]{2,1,0:T(8,128)(2,1)S(1)}, u32[]{:S(2)}, u32[]{:S(2)}) collective-permute-start(bf16[16,32,640]{2,1,0:T(8,128)(2,1)S(1)} %add_convert_fusion.2), channel_id=1, source_target_pairs={{0,2},{1,3},{2,0},{3,1},{4,6},{5,7},{6,4},{7,5},{8,10},{9,11},{10,... | collective-permute-start | bytes 1966088 | tf_op jit(solution)/shard_map/ppermute | solution.py:333
  194.4 31.5 %copy-start = (bf16[16,32,640]{2,1,0:T(8,128)(2,1)S(1)}, bf16[16,32,640]{2,1,0:T(8,128)(2,1)}, u32[]{:S(2)}) copy-start(bf16[16,32,640]{2,1,0:T(8,128)(2,1)} %get-tuple-element.26.p0) | copy-start | bytes 1966084
  194.4 31.5 %collective-permute-start.23 = (bf16[16,32,640]{2,1,0:T(8,128)(2,1)S(1)}, bf16[16,32,640]{2,1,0:T(8,128)(2,1)S(1)}, u32[]{:S(2)}, u32[]{:S(2)}) collective-permute-start(bf16[16,32,640]{2,1,0:T(8,128)(2,1)S(1)} %add_convert_fusion.1), channel_id=1, source_target_pairs={{0,1},{1,2},{2,3},{3,0},{4,5},{5,6},{6,7},{7,4},{8,9},{9,10},{10,1... | collective-permute-start | bytes 1966088 | tf_op jit(solution)/shard_map/ppermute | solution.py:333
  196.1 29.8 %collective-permute-start.25 = (bf16[16,32,640]{2,1,0:T(8,128)(2,1)S(1)}, bf16[16,32,640]{2,1,0:T(8,128)(2,1)S(1)}, u32[]{:S(2)}, u32[]{:S(2)}) collective-permute-start(bf16[16,32,640]{2,1,0:T(8,128)(2,1)S(1)} %add_convert_fusion), channel_id=1, source_target_pairs={{0,3},{1,0},{2,1},{3,2},{4,7},{5,4},{6,5},{7,6},{8,11},{9,8},{10,9... | collective-permute-start | bytes 1966088 | tf_op jit(solution)/shard_map/ppermute | solution.py:333
  227.3 31.0 %all-to-all-start.1 = ((bf16[32,32,384]{2,1,0:T(8,128)(2,1)}), bf16[32,32,384]{2,1,0:T(8,128)(2,1)S(1)}, u32[]{:S(2)}, u32[]{:S(2)}) async-start(bf16[32,32,384]{2,1,0:T(8,128)(2,1)} %bitcast.18), calls=%async_computation.1 | async-start | bytes 1572864 | tf_op jit(solution)/shard_map/all_to_all | solution.py:375
  236.5 20.4 %collective-permute-start.29 = (f32[40,640]{1,0:T(8,128)S(1)}, f32[40,640]{1,0:T(8,128)S(1)}, u32[]{:S(2)}, u32[]{:S(2)}) collective-permute-start(f32[40,640]{1,0:T(8,128)S(1)} %broadcast_multiply_fusion), channel_id=1, source_target_pairs={{0,0},{4,8},{8,4},{12,12},{1,1},{5,9},{9,5},{13,13},{2,2},{6,10},{... | collective-permute-start | bytes 307208 | tf_op jit(solution)/shard_map/ppermute | solution.py:337
